TPU v7x, 256 devices: a whole 4x4x8 slice. The times are simulated.
256 devices in a mesh: crop: 2 (over core), row: 8 (over x_hi, y), col: 16 (over z, x_lo).
Axes of the slice: x: 4 (x_hi: 2, x_lo: 2; x = x_hi * 2 + x_lo), y: 4, z: 8, core: 2. Of those that a mesh axis runs over, the one named last changes fastest.
Arguments:
- pair_state: bfloat16 [768, 384, 128], P(('crop', 'row'), 'col'), parts along dimension 0, may hold values from -6 to 6
- token_mask: int32 [768], P('crop'), parts along dimension 0, may hold values from 0 to 1, as said below
- block_pattern: int32 [8, 4], P('crop'), parts along dimension 0, may hold values from 0 to 1, as said below
- triangle_norm: float32 [128], replicated, may hold values from 0.1 to 1.9
- triangle_input: bfloat16 [128, 512], replicated, may hold values from -0.5 to 0.5
- triangle_gate: bfloat16 [128, 128], replicated, may hold values from -0.5 to 0.5
- product_norm: float32 [128], replicated, may hold values from 0.1 to 1.9
- triangle_output: bfloat16 [128, 128], replicated, may hold values from -0.5 to 0.5
- attend_norm: float32 [128], replicated, may hold values from 0.1 to 1.9
- attend_inputs: bfloat16 [128, 384], replicated, may hold values from -4 to 4
- attend_gate: bfloat16 [128, 128], replicated, may hold values from -0.5 to 0.5
- attend_bias: bfloat16 [128, 4], replicated, may hold values from -0.5 to 0.5
- attend_output: bfloat16 [128, 128], replicated, may hold values from -0.5 to 0.5
Outputs:
- pair_output: bfloat16 [768, 384, 128], P(('crop', 'row'), 'col'), parts along dimension 0
There are 2 independent parts, one for each index of `crop`. A program takes and returns all parts, laid end to end along the dimension named above; an argument that names none is the same for every part. Nothing has to cross between parts.
Inputs may be any that keep to these rules, and one draw needn't show every extreme that they name: `token_mask`: 1 on a prefix of 96 or more tokens and 0 after it. `block_pattern`: every row allows its own block and block 0.
All inputs are finite; a program needn't handle non-finite values.
Results may differ from a plain program's by a relative error of at most 0.02.
Values may be sent and summed in bfloat16 or wider, within the bound.
A program may use at most 64 MiB of HBM per device.

v0:
```python
import math
import jax
import jax.numpy as jnp
from jax import lax
from jax.sharding import Mesh
from jax.sharding import PartitionSpec as P

ROW = ("row_0", "row_1")
COL = ("col_0", "col_1")
ROW_COL = ("row_0", "row_1", "col_0", "col_1")
CROP_ROW = ("crop", "row_0", "row_1")
norm_epsilon = 1e-05


def joined_along(pieces, dim):
    lengths = list(pieces.shape[1:])
    lengths[dim] *= pieces.shape[0]
    return jnp.moveaxis(pieces, 0, dim).reshape(lengths)


def gather_in_order(array, axes, turns):
    pieces = array[None]
    for k in turns:
        pieces = lax.all_gather(pieces, axes[k], axis=0, tiled=True)
    held = [lax.axis_size(axes[k]) for k in reversed(turns)]
    pieces = pieces.reshape(*held, *array.shape)
    turned = sorted(range(len(turns)), key=lambda place: turns[len(turns) - 1 - place])
    return pieces.transpose(*turned, *range(len(turns), pieces.ndim)).reshape(-1, *array.shape)


def whole_of(array, axes, turns, dim):
    return joined_along(gather_in_order(array, axes, turns), dim)


def layer_norm(inputs, gain):
    average = jnp.mean(inputs, axis=-1, keepdims=True)
    centered = inputs - average
    variance = jnp.mean(centered * centered, axis=-1, keepdims=True)
    return centered * lax.rsqrt(variance + norm_epsilon) * gain


def project_rows(pair_rows, attend_inputs, attend_gate, head_count):
    row_count, token_count, channels = pair_rows.shape
    head_width = channels // head_count
    combined = jnp.dot(pair_rows, attend_inputs, preferred_element_type=jnp.float32)
    queries = (
        combined[..., :channels]
        .astype(jnp.bfloat16)
        .reshape(row_count, token_count, head_count, head_width)
    )
    key_rows = (
        combined[..., channels : 2 * channels]
        .astype(jnp.bfloat16)
        .reshape(row_count, token_count, head_count, head_width)
    )
    values = (
        combined[..., 2 * channels :]
        .astype(jnp.bfloat16)
        .reshape(row_count, token_count, head_count, head_width)
    )
    gate_values = jax.nn.sigmoid(
        jnp.dot(pair_rows, attend_gate, preferred_element_type=jnp.float32)
    )
    return (queries, key_rows, values, gate_values)


def attend_dense(pair_rows, attend_inputs, attend_gate, head_bias, allowed):
    row_count, token_count, channels = pair_rows.shape
    head_count = head_bias.shape[0]
    queries, key_rows, values, gate_values = project_rows(
        pair_rows, attend_inputs, attend_gate, head_count
    )
    scores = jnp.einsum(
        "rjhd,rkhd->rhjk", queries, key_rows, preferred_element_type=jnp.float32
    ) / math.sqrt(channels // head_count)
    scores = scores + head_bias.astype(jnp.float32)[None]
    scores = jnp.where(allowed[None, None], scores, -jnp.inf)
    row_max = jnp.max(scores, axis=-1, keepdims=True)
    weights = jnp.exp(scores - row_max)
    probabilities = (weights / jnp.sum(weights, axis=-1, keepdims=True)).astype(jnp.bfloat16)
    attended = jnp.einsum(
        "rhjk,rkhd->rjhd", probabilities, values, preferred_element_type=jnp.float32
    ).reshape(row_count, token_count, channels)
    return (gate_values * attended).astype(jnp.bfloat16)


def shards(
    pair_state,
    token_mask,
    block_pattern,
    triangle_norm,
    triangle_input,
    triangle_gate,
    product_norm,
    triangle_output,
    attend_norm,
    attend_inputs,
    attend_gate,
    attend_bias,
    attend_output,
):
    tile_rows, tile_columns, channels = pair_state.shape
    row_devices = lax.axis_size(ROW)
    column_devices = lax.axis_size(COL)
    token_count = tile_columns * column_devices
    row_index = lax.axis_index(ROW)
    column_index = lax.axis_index(COL)
    valid_tokens = token_mask.astype(jnp.float32)
    row_valid = lax.dynamic_slice_in_dim(valid_tokens, row_index * tile_rows, tile_rows)
    column_valid = lax.dynamic_slice_in_dim(valid_tokens, column_index * tile_columns, tile_columns)
    state_float = pair_state.astype(jnp.float32)
    normed = layer_norm(state_float, triangle_norm).astype(jnp.bfloat16)
    projected = jnp.dot(normed, triangle_input, preferred_element_type=jnp.float32)
    pair_valid = (row_valid[:, None] * column_valid[None, :])[:, :, None]
    left_factor = (
        pair_valid
        * jax.nn.sigmoid(projected[..., :channels])
        * projected[..., channels : 2 * channels]
    ).astype(jnp.bfloat16)
    right_factor = (
        pair_valid
        * jax.nn.sigmoid(projected[..., 2 * channels : 3 * channels])
        * projected[..., 3 * channels :]
    ).astype(jnp.bfloat16)
    right_columns = lax.all_gather(right_factor, ROW, axis=0, tiled=True)
    summed_part = lax.dot_general(
        right_columns, left_factor, (((1,), (1,)), ((2,), (2,))), preferred_element_type=jnp.float32
    )
    flipped = lax.psum_scatter(
        jnp.transpose(summed_part, (1, 2, 0)), COL, scatter_dimension=0, tiled=True
    )
    product = jnp.transpose(flipped, (1, 0, 2))
    product_normed = layer_norm(product, product_norm).astype(jnp.bfloat16)
    gate_values = jax.nn.sigmoid(jnp.dot(normed, triangle_gate, preferred_element_type=jnp.float32))
    middle = (
        state_float
        + gate_values * jnp.dot(product_normed, triangle_output, preferred_element_type=jnp.float32)
    ).astype(jnp.bfloat16)
    attend_normed = layer_norm(middle.astype(jnp.float32), attend_norm).astype(jnp.bfloat16)
    head_count = attend_bias.shape[1]
    bias_tile = jnp.dot(attend_normed, attend_bias, preferred_element_type=jnp.float32).astype(
        jnp.bfloat16
    )
    flat_bias = jnp.transpose(bias_tile, (2, 0, 1)).reshape(head_count, tile_rows * tile_columns)
    gathered = whole_of(flat_bias, ROW_COL, (0, 3, 1, 2), 1)
    head_bias = gathered.reshape(head_count, row_devices, column_devices, tile_rows, tile_columns)
    head_bias = jnp.transpose(head_bias, (0, 1, 3, 2, 4)).reshape(
        head_count, token_count, token_count
    )
    blocks = block_pattern.shape[0]
    block_width = token_count // blocks
    pattern_ok = block_pattern[:, None, :, None] > 0
    allowed = jnp.broadcast_to(pattern_ok, (blocks, block_width, blocks, block_width)).reshape(
        token_count, token_count
    ) & (token_mask[None, :] > 0)
    rows_each = tile_rows // column_devices
    grouped = attend_normed.reshape(column_devices, rows_each, tile_columns, channels)
    received = lax.all_to_all(grouped, COL, split_axis=0, concat_axis=2, tiled=True)
    outer, inner, tokens_here, width_here = received.shape
    flat = received.reshape(outer * inner, tokens_here, width_here)
    attended_rows = attend_dense(flat, attend_inputs, attend_gate, head_bias, allowed).reshape(
        outer, inner, tokens_here, width_here
    )
    returned = lax.all_to_all(attended_rows, COL, split_axis=2, concat_axis=0, tiled=True)
    returned = returned.reshape(tile_rows, tile_columns, channels)
    update = jnp.dot(returned, attend_output, preferred_element_type=jnp.float32)
    return (middle.astype(jnp.float32) + update).astype(jnp.bfloat16)


def solution(mesh):
    finer = Mesh(
        mesh.devices.reshape(mesh.shape["crop"], 2, 4, 8, 2),
        ("crop", "row_0", "row_1", "col_0", "col_1"),
    )
    return jax.shard_map(
        shards,
        mesh=finer,
        in_specs=(
            P(CROP_ROW, COL, None),
            P("crop"),
            P("crop", None),
            P(),
            P(),
            P(),
            P(),
            P(),
            P(),
            P(),
            P(),
            P(),
            P(),
        ),
        out_specs=P(CROP_ROW, COL, None),
        check_vma=False,
    )
```

profile of v0, /device:TPU:8, one launch (start us, length us, event | category | flops | bytes accessed | tf_op | source)
XLA Modules:
  0.0 430.4 jit_solution(2989985232182543160)
XLA Ops:
  6.5 0.7 convert_element_type.68
  7.4 1.2 convert_reduce_fusion
  8.6 1.4 fusion.25
  10.1 1.5 fusion.39
  11.6 1.1 fusion.28
  13.2 61.9 %all-gather.3.cloned.1.call-done = bf16[384,24,128]{2,1,0:T(8,128)(2,1)} async-done(((bf16[48,24,128]{2,1,0:T(8,128)(2,1)}), bf16[384,24,128]{2,1,0:T(8,128)(2,1)}) %all-gather.3.cloned.1.call-update) | async-done | bytes 2359312 | tf_op jit(solution)/shard_map/all_gather | solution.py:125
  75.1 3.7 copy.84
  78.8 5.1 %convolution_bitcast_fusion = f32[384,48,128]{0,1,2:T(8,128)} fusion(bf16[384,24,128]{0,1,2:T(8,128)(2,1)S(1)} %copy.84, bf16[48,24,128]{0,1,2:T(8,128)(2,1)S(1)} %copy.85), kind=kOutput, calls=%fused_computation.10 | convolution fusion | flops 113246208 | bytes 12091392 | tf_op jit(solution)/shard_map/dot_general | solution.py:126
  83.9 9.8 %copy.86 = f32[384,48,128]{2,1,0:T(8,128)} copy(f32[384,48,128]{0,1,2:T(8,128)} %convolution_bitcast_fusion) | data formatting | bytes 18874368 | tf_op jit(solution)/shard_map/transpose | solution.py:130
  93.9 0.8 copy-done.2
  94.7 0.5 fusion.14
  95.2 201.7 %reduce-scatter.2.cloned.1.call-done = f32[24,48,128]{2,1,0:T(8,128)} async-done(((f32[384,48,128]{2,1,0:T(8,128)}), f32[24,48,128]{2,1,0:T(8,128)}) %reduce-scatter.2.cloned.1.call-update) | async-done | bytes 589840 | tf_op jit(solution)/shard_map/reduce_scatter | solution.py:129
  296.9 1.3 bitcast_reduce_fusion
  298.4 1.5 multiply_reduce_fusion.1
  300.0 1.4 multiply_convert_fusion.1
  302.3 1.1 multiply_convert_fusion
  303.4 1.6 fusion.20
  305.1 5.9 %all_gather.16 = bf16[2,4,1152]{2,1,0:T(4,128)(2,1)S(1)} all-gather(bf16[1,4,1152]{2,1,0:T(4,128)(2,1)S(1)} %broadcast_in_dim_reshape.3), channel_id=1, replica_groups=mesh['crop'=2,'row_0'=2,'row_1'=4,'col_0'=8,'col_1'=2] {'row_0'}, dimensions={0}, use_global_device_ids=true | all-gather | bytes 27648 | tf_op jit(solution)/shard_map/all_gather | solution.py:24
  311.0 4.4 %all_gather.17 = bf16[4,4,1152]{2,1,0:T(4,128)(2,1)S(1)} all-gather(bf16[2,4,1152]{2,1,0:T(4,128)(2,1)S(1)} %all_gather.16), channel_id=1, replica_groups=mesh['crop'=2,'row_0'=2,'row_1'=4,'col_0'=8,'col_1'=2] {'col_1'}, dimensions={0}, use_global_device_ids=true | all-gather | bytes 55296 | tf_op jit(solution)/shard_map/all_gather | solution.py:24
  315.4 12.8 %all_gather.18 = bf16[16,4,1152]{2,1,0:T(4,128)(2,1)} all-gather(bf16[4,4,1152]{2,1,0:T(4,128)(2,1)S(1)} %all_gather.17), channel_id=1, replica_groups=mesh['crop'=2,'row_0'=2,'row_1'=4,'col_0'=8,'col_1'=2] {'row_1'}, dimensions={0}, use_global_device_ids=true | all-gather | bytes 184320 | tf_op jit(solution)/shard_map/all_gather | solution.py:24
  328.3 7.1 %all-to-all-start = ((bf16[16,3,24,128]{3,2,1,0:T(8,128)(2,1)}), bf16[16,3,24,128]{3,2,1,0:T(8,128)(2,1)S(1)}, u32[]{:S(2)}, u32[]{:S(2)}) async-start(bf16[16,3,24,128]{3,2,1,0:T(8,128)(2,1)} %bitcast.5), calls=%async_computation.1 | async-start | bytes 589824 | tf_op jit(solution)/shard_map/all_to_all | solution.py:158
  336.2 10.3 %all-to-all-done = bf16[16,3,24,128]{3,2,1,0:T(8,128)(2,1)S(1)} async-done(((bf16[16,3,24,128]{3,2,1,0:T(8,128)(2,1)}), bf16[16,3,24,128]{3,2,1,0:T(8,128)(2,1)S(1)}, u32[]{:S(2)}, u32[]{:S(2)}) %all-to-all-start) | async-done | bytes 294944 | tf_op jit(solution)/shard_map/all_to_all | solution.py:158
  347.0 0.9 fusion.51
  348.0 19.6 %all-gather.5.cloned.1.call-done = bf16[128,4,1152]{2,1,0:T(4,128)(2,1)} async-done(((bf16[16,4,1152]{2,1,0:T(4,128)(2,1)}), bf16[128,4,1152]{2,1,0:T(4,128)(2,1)}) %all-gather.5.cloned.1.call-update) | async-done | bytes 1179664 | tf_op jit(solution)/shard_map/all_gather | solution.py:24
  367.6 1.7 copy.96
  369.5 9.5 %reshape.148 = f32[4,8,16,48,24]{4,3,2,1,0:T(8,128)} reshape(f32[4,128,1152]{2,1,0:T(8,128)S(1)} %copy.97) | data formatting | bytes 4718592 | tf_op jit(solution)/shard_map/convert_element_type | solution.py:76
  379.0 10.7 %copy.98 = f32[4,8,48,16,24]{2,1,4,3,0:T(8,128)} copy(f32[4,8,48,16,24]{4,2,3,1,0:T(8,128)} %bitcast.76) | data formatting | bytes 4718592 | tf_op jit(solution)/shard_map/convert_element_type | solution.py:76
  389.7 4.8 %reshape.147 = f32[4,384,384]{1,2,0:T(8,128)S(1)} reshape(f32[4,8,48,16,24]{2,1,4,3,0:T(8,128)} %copy.98) | data formatting | bytes 4718592 | tf_op jit(solution)/shard_map/convert_element_type | solution.py:76
  394.4 6.6 %fusion.53 = (f32[3,4,384]{2,1,0:T(4,128)S(1)}, f32[3,4,384,384]{2,3,1,0:T(8,128)}) fusion(f32[4,384,384]{1,2,0:T(8,128)S(1)} %reshape.147, pred[384,384]{0,1:T(8,128)(4,1)S(1)} %broadcast_and_fusion, bf16[3,384,4,32]{1,3,2,0:T(8,128)(2,1)} %bitcast.87, bf16[3,384,4,32]{1,3,2,0:T(8,128)(2,1)} %bitcast.86), kind=kOutput, calls=%fused_computation.82 | convolution fusion | flops 122093952 | bytes 10192896 | tf_op jit(solution)/shard_map/sub | solution.py:79
  401.1 3.8 fusion.6
  405.7 17.1 %all_to_all.30 = bf16[1,3,384,128]{3,1,0,2:T(4,128)(2,1)S(1)} all-to-all(bf16[1,3,384,128]{3,1,0,2:T(4,128)(2,1)S(1)} %copy.101), channel_id=1, replica_groups=mesh['crop'=2,'row_0'=2,'row_1'=4,'col_0'=8,'col_1'=2] {'col_0','col_1'}, dimensions={2} | all-to-all | bytes 589824 | tf_op jit(solution)/shard_map/all_to_all | solution.py:164
  422.8 1.0 fusion.18
  (64 shorter events, 4.4 us)
Async XLA Ops:
  6.5 3.5 copy-start
  6.5 68.6 %all-gather.3.cloned.1.call-start = ((), (), s32[]{:S(2)}) async-start(), calls=%async_computation.3 | async-start | bytes 2654208 | tf_op jit(solution)/shard_map/all_gather | solution.py:125
  12.7 284.2 %reduce-scatter.2.cloned.1.call-start = ((), (), s32[]{:S(2)}) async-start(), calls=%async_computation.4 | async-start | bytes 10027008 | tf_op jit(solution)/shard_map/reduce_scatter | solution.py:129
  93.7 1.0 copy-start.2
  93.7 1.0 copy-start.9
  93.7 1.0 copy-start.12
  93.7 206.3 %copy-start.10 = (f32[128]{0:T(128)S(1)}, f32[128]{0:T(128)}, u32[]{:S(2)}) copy-start(f32[128]{0:T(128)} %param.19) | copy-start | bytes 1540
  93.7 207.7 %copy-start.4 = (bf16[128,128]{1,0:T(8,128)(2,1)S(1)}, bf16[128,128]{1,0:T(8,128)(2,1)}, u32[]{:S(2)}) copy-start(bf16[128,128]{1,0:T(8,128)(2,1)} %param.20) | copy-start | bytes 98308
  93.8 208.6 %copy-start.11 = (f32[128]{0:T(128)S(1)}, f32[128]{0:T(128)}, u32[]{:S(2)}) copy-start(f32[128]{0:T(128)} %param.21) | copy-start | bytes 1540
  93.8 209.7 %copy-start.8 = (bf16[128,4]{0,1:T(4,128)(2,1)S(1)}, bf16[128,4]{0,1:T(4,128)(2,1)}, u32[]{:S(2)}) copy-start(bf16[128,4]{0,1:T(4,128)(2,1)} %param.24) | copy-start | bytes 3076
  93.8 241.6 %copy-start.7 = (s32[4,4]{1,0:T(4,128)S(1)}, s32[4,4]{1,0:T(4,128)}, u32[]{:S(2)}) copy-start(s32[4,4]{1,0:T(4,128)} %param.15) | copy-start | bytes 196
  93.8 242.2 %copy-start.6 = (s32[384]{0:T(512)S(1)}, s32[384]{0:T(512)}, u32[]{:S(2)}) copy-start(s32[384]{0:T(512)} %param.14) | copy-start | bytes 4612
  93.8 252.7 %copy-start.3 = (bf16[128,384]{1,0:T(8,128)(2,1)S(1)}, bf16[128,384]{1,0:T(8,128)(2,1)}, u32[]{:S(2)}) copy-start(bf16[128,384]{1,0:T(8,128)(2,1)} %param.22) | copy-start | bytes 294916
  93.8 273.8 %all-gather.5.cloned.1.call-start = ((), (), s32[]{:S(2)}) async-start(), calls=%async_computation.5 | async-start | bytes 1327104 | tf_op jit(solution)/shard_map/all_gather | solution.py:24
  328.3 18.3 %all-to-all-start = ((bf16[16,3,24,128]{3,2,1,0:T(8,128)(2,1)}), bf16[16,3,24,128]{3,2,1,0:T(8,128)(2,1)S(1)}, u32[]{:S(2)}, u32[]{:S(2)}) async-start(bf16[16,3,24,128]{3,2,1,0:T(8,128)(2,1)} %bitcast.5), calls=%async_computation.1 | async-start | bytes 589824 | tf_op jit(solution)/shard_map/all_to_all | solution.py:158
  401.0 4.0 copy-start.13
  401.0 21.8 %copy-start.5 = (bf16[128,128]{1,0:T(8,128)(2,1)S(1)}, bf16[128,128]{1,0:T(8,128)(2,1)}, u32[]{:S(2)}) copy-start(bf16[128,128]{1,0:T(8,128)(2,1)} %param.25) | copy-start | bytes 98308
  401.1 22.8 %copy-start.1 = (bf16[128,512]{1,0:T(8,128)(2,1)S(1)}, bf16[128,512]{1,0:T(8,128)(2,1)}, u32[]{:S(2)}) copy-start(bf16[128,512]{1,0:T(8,128)(2,1)} %param.17) | copy-start | bytes 393220
Sparse Core Ops, SparseCore 0:
  12.8 62.2 all-gather.2
  93.9 202.9 reduce-scatter.1
  328.4 39.1 all-gather.4
where the time goes:
time: 431 us; the launch traced here: 430 us
  waiting for transfers between devices  294 us (68%)
  local copies, waits for them, and re-layouts  44.4 us (10%)
  blocking collectives  40.2 us (9%)
  matrix products  21.2 us (5%)
  between operations  13.5 us (3%)
  other arithmetic  10.3 us (2%)
  starting transfers between devices  7.23 us (2%)
    reduce_scatter x1, waiting for transfers between devices, shards(): lax.psum_scatter(jnp.transpose(summed_part, (1, 2, 0)), COL, scatter_dime...  202 us
    all_gather x1, waiting for transfers between devices, shards(): right_columns = lax.all_gather(right_factor, ROW, axis=0, tiled=True)  61.9 us
    convert_element_type x5, local copies, waits for them, and re-layouts, attend_dense(): scores = scores + head_bias.astype(jnp.float32)[None]  26.8 us
    all_gather x3, blocking collectives, gather_in_order(): pieces = lax.all_gather(pieces, axes[k], axis=0, tiled=True)  23.1 us
    all_gather x1, waiting for transfers between devices, gather_in_order(): pieces = lax.all_gather(pieces, axes[k], axis=0, tiled=True)  19.6 us
    all_to_all x1, blocking collectives, shards(): lax.all_to_all(attended_rows, COL, split_axis=2, concat_axis=0, tiled=True)  17.1 us
    all_to_all x1, waiting for transfers between devices, shards(): lax.all_to_all(grouped, COL, split_axis=0, concat_axis=2, tiled=True)  10.3 us
    transpose x1, local copies, waits for them, and re-layouts, shards(): jnp.transpose(summed_part, (1, 2, 0))  9.81 us
  transfers between devices with their start and end apart: 4, of which 4 were waited for; matrix products, arithmetic and copies ran while one was open for 1% of the time, Pallas kernels for 0%

commit v1 on v0

--- a/solution.py
+++ b/solution.py
@@ -122,7 +122,9 @@
         * jax.nn.sigmoid(projected[..., 2 * channels : 3 * channels])
         * projected[..., 3 * channels :]
     ).astype(jnp.bfloat16)
-    right_columns = lax.all_gather(right_factor, ROW, axis=0, tiled=True)
+    right_columns = jnp.concatenate(
+        lax.all_to_all(jnp.stack([right_factor] * lax.axis_size(ROW)), ROW, 0, 0), axis=0
+    )
     summed_part = lax.dot_general(
         right_columns, left_factor, (((1,), (1,)), ((2,), (2,))), preferred_element_type=jnp.float32
     )

time: 431 us -> 410 us (0.951)
  waiting for transfers between devices: 294 us -> 260 us
  starting transfers between devices: 7.23 us -> 14.6 us
    all_gather x1 -> x0, waiting for transfers between devices: 61.9 us -> none  [shards(): right_columns = lax.all_gather(right_factor, ROW, axis=0, tiled=True)]
    all_to_all x0 -> x1, waiting for transfers between devices: none -> 27.1 us  [shards(): lax.all_to_all(jnp.stack([right_factor] * lax.axis_size(ROW)), ROW, 0, 0)]
    all_to_all x0 -> x1, starting transfers between devices: none -> 7.37 us  [shards(): lax.all_to_all(jnp.stack([right_factor] * lax.axis_size(ROW)), ROW, 0, 0)]
where the time goes in v1:
time: 410 us; the launch traced here: 409 us
  waiting for transfers between devices  260 us (63%)
  local copies, waits for them, and re-layouts  46.8 us (11%)
  blocking collectives  40.2 us (10%)
  matrix products  22.9 us (6%)
  starting transfers between devices  14.6 us (4%)
  between operations  13.7 us (3%)
  other arithmetic  10.3 us (3%)
    reduce_scatter x1, waiting for transfers between devices, shards(): lax.psum_scatter(jnp.transpose(summed_part, (1, 2, 0)), COL, scatter_dime...  203 us
    all_to_all x1, waiting for transfers between devices, shards(): lax.all_to_all(jnp.stack([right_factor] * lax.axis_size(ROW)), ROW, 0, 0)  27.1 us
    convert_element_type x5, local copies, waits for them, and re-layouts, attend_dense(): scores = scores + head_bias.astype(jnp.float32)[None]  26.8 us
    all_gather x3, blocking collectives, gather_in_order(): pieces = lax.all_gather(pieces, axes[k], axis=0, tiled=True)  23.1 us
    all_gather x1, waiting for transfers between devices, gather_in_order(): pieces = lax.all_gather(pieces, axes[k], axis=0, tiled=True)  19.6 us
    all_to_all x1, blocking collectives, shards(): lax.all_to_all(attended_rows, COL, split_axis=2, concat_axis=0, tiled=True)  17.1 us
    all_to_all x1, waiting for transfers between devices, shards(): lax.all_to_all(grouped, COL, split_axis=0, concat_axis=2, tiled=True)  10.3 us
    transpose x1, local copies, waits for them, and re-layouts, shards(): jnp.transpose(summed_part, (1, 2, 0))  9.78 us
  transfers between devices with their start and end apart: 4, of which 4 were waited for; matrix products, arithmetic and copies ran while one was open for 1% of the time, Pallas kernels for 0%

profile of v1, /device:TPU:8, one launch (start us, length us, event | category | flops | bytes accessed | tf_op | source)
XLA Modules:
  0.0 408.9 jit_solution(8401492152655466099)
XLA Ops:
  7.4 1.2 convert_reduce_fusion
  8.6 1.4 fusion.25
  10.1 1.5 fusion.39
  11.6 1.1 fusion.28
  12.7 1.7 stack.2
  14.4 7.4 %all-to-all-start = ((bf16[8,48,24,128]{3,2,1,0:T(8,128)(2,1)}), bf16[8,48,24,128]{3,2,1,0:T(8,128)(2,1)S(1)}, u32[]{:S(2)}, u32[]{:S(2)}) async-start(bf16[8,48,24,128]{3,2,1,0:T(8,128)(2,1)} %stack.2), calls=%async_computation | async-start | bytes 4718592 | tf_op jit(solution)/shard_map/all_to_all | solution.py:126
  21.8 1.5 copy.85
  23.3 27.1 %all-to-all-done = bf16[8,48,24,128]{3,2,1,0:T(8,128)(2,1)S(1)} async-done(((bf16[8,48,24,128]{3,2,1,0:T(8,128)(2,1)}), bf16[8,48,24,128]{3,2,1,0:T(8,128)(2,1)S(1)}, u32[]{:S(2)}, u32[]{:S(2)}) %all-to-all-start) | async-done | bytes 2359328 | tf_op jit(solution)/shard_map/all_to_all | solution.py:126
  50.4 3.4 copy.84
  53.8 6.7 %convolution_bitcast_fusion = f32[384,48,128]{0,1,2:T(8,128)} fusion(bf16[384,24,128]{0,1,2:T(8,128)(2,1)} %copy.84, bf16[48,24,128]{0,1,2:T(8,128)(2,1)S(1)} %copy.85), kind=kOutput, calls=%fused_computation.10 | convolution fusion | flops 113246208 | bytes 12091392 | tf_op jit(solution)/shard_map/dot_general | solution.py:128
  60.5 9.8 %copy.86 = f32[384,48,128]{2,1,0:T(8,128)} copy(f32[384,48,128]{0,1,2:T(8,128)} %convolution_bitcast_fusion) | data formatting | bytes 18874368 | tf_op jit(solution)/shard_map/transpose | solution.py:132
  71.8 203.3 %reduce-scatter.2.cloned.1.call-done = f32[24,48,128]{2,1,0:T(8,128)} async-done(((f32[384,48,128]{2,1,0:T(8,128)}), f32[24,48,128]{2,1,0:T(8,128)}) %reduce-scatter.2.cloned.1.call-update) | async-done | bytes 589840 | tf_op jit(solution)/shard_map/reduce_scatter | solution.py:131
  275.1 1.3 bitcast_reduce_fusion
  276.6 1.5 multiply_reduce_fusion.1
  278.2 1.4 multiply_convert_fusion.1
  280.5 1.1 multiply_convert_fusion
  281.6 1.6 fusion.20
  283.3 5.9 %all_gather.12 = bf16[2,4,1152]{2,1,0:T(4,128)(2,1)S(1)} all-gather(bf16[1,4,1152]{2,1,0:T(4,128)(2,1)S(1)} %broadcast_in_dim_reshape.3), channel_id=1, replica_groups=mesh['crop'=2,'row_0'=2,'row_1'=4,'col_0'=8,'col_1'=2] {'row_0'}, dimensions={0}, use_global_device_ids=true | all-gather | bytes 27648 | tf_op jit(solution)/shard_map/all_gather | solution.py:24
  289.2 4.4 %all_gather.13 = bf16[4,4,1152]{2,1,0:T(4,128)(2,1)S(1)} all-gather(bf16[2,4,1152]{2,1,0:T(4,128)(2,1)S(1)} %all_gather.12), channel_id=1, replica_groups=mesh['crop'=2,'row_0'=2,'row_1'=4,'col_0'=8,'col_1'=2] {'col_1'}, dimensions={0}, use_global_device_ids=true | all-gather | bytes 55296 | tf_op jit(solution)/shard_map/all_gather | solution.py:24
  293.6 12.8 %all_gather.14 = bf16[16,4,1152]{2,1,0:T(4,128)(2,1)} all-gather(bf16[4,4,1152]{2,1,0:T(4,128)(2,1)S(1)} %all_gather.13), channel_id=1, replica_groups=mesh['crop'=2,'row_0'=2,'row_1'=4,'col_0'=8,'col_1'=2] {'row_1'}, dimensions={0}, use_global_device_ids=true | all-gather | bytes 184320 | tf_op jit(solution)/shard_map/all_gather | solution.py:24
  306.5 7.1 %all-to-all-start.1 = ((bf16[16,3,24,128]{3,2,1,0:T(8,128)(2,1)}), bf16[16,3,24,128]{3,2,1,0:T(8,128)(2,1)S(1)}, u32[]{:S(2)}, u32[]{:S(2)}) async-start(bf16[16,3,24,128]{3,2,1,0:T(8,128)(2,1)} %bitcast.6), calls=%async_computation.2 | async-start | bytes 589824 | tf_op jit(solution)/shard_map/all_to_all | solution.py:160
  314.4 10.3 %all-to-all-done.1 = bf16[16,3,24,128]{3,2,1,0:T(8,128)(2,1)S(1)} async-done(((bf16[16,3,24,128]{3,2,1,0:T(8,128)(2,1)}), bf16[16,3,24,128]{3,2,1,0:T(8,128)(2,1)S(1)}, u32[]{:S(2)}, u32[]{:S(2)}) %all-to-all-start.1) | async-done | bytes 294944 | tf_op jit(solution)/shard_map/all_to_all | solution.py:160
  325.2 0.9 fusion.51
  326.2 19.6 %all-gather.2.cloned.1.call-done = bf16[128,4,1152]{2,1,0:T(4,128)(2,1)} async-done(((bf16[16,4,1152]{2,1,0:T(4,128)(2,1)}), bf16[128,4,1152]{2,1,0:T(4,128)(2,1)}) %all-gather.2.cloned.1.call-update) | async-done | bytes 1179664 | tf_op jit(solution)/shard_map/all_gather | solution.py:24
  345.8 1.7 copy.96
  347.7 9.5 %reshape.154 = f32[4,8,16,48,24]{4,3,2,1,0:T(8,128)} reshape(f32[4,128,1152]{2,1,0:T(8,128)S(1)} %copy.97) | data formatting | bytes 4718592 | tf_op jit(solution)/shard_map/convert_element_type | solution.py:76
  357.2 10.7 %copy.98 = f32[4,8,48,16,24]{2,1,4,3,0:T(8,128)} copy(f32[4,8,48,16,24]{4,2,3,1,0:T(8,128)} %bitcast.77) | data formatting | bytes 4718592 | tf_op jit(solution)/shard_map/convert_element_type | solution.py:76
  367.9 4.8 %reshape.153 = f32[4,384,384]{1,2,0:T(8,128)S(1)} reshape(f32[4,8,48,16,24]{2,1,4,3,0:T(8,128)} %copy.98) | data formatting | bytes 4718592 | tf_op jit(solution)/shard_map/convert_element_type | solution.py:76
  372.7 6.6 %fusion.53 = (f32[3,4,384]{2,1,0:T(4,128)S(1)}, f32[3,4,384,384]{2,3,1,0:T(8,128)}) fusion(f32[4,384,384]{1,2,0:T(8,128)S(1)} %reshape.153, pred[384,384]{0,1:T(8,128)(4,1)S(1)} %broadcast_and_fusion, bf16[3,384,4,32]{1,3,2,0:T(8,128)(2,1)} %bitcast.89, bf16[3,384,4,32]{1,3,2,0:T(8,128)(2,1)} %bitcast.88), kind=kOutput, calls=%fused_computation.82 | convolution fusion | flops 122093952 | bytes 10192896 | tf_op jit(solution)/shard_map/sub | solution.py:79
  379.3 3.8 fusion.6
  383.9 17.1 %all_to_all.35 = bf16[1,3,384,128]{3,1,0,2:T(4,128)(2,1)S(1)} all-to-all(bf16[1,3,384,128]{3,1,0,2:T(4,128)(2,1)S(1)} %copy.101), channel_id=1, replica_groups=mesh['crop'=2,'row_0'=2,'row_1'=4,'col_0'=8,'col_1'=2] {'col_0','col_1'}, dimensions={2} | all-to-all | bytes 589824 | tf_op jit(solution)/shard_map/all_to_all | solution.py:166
  401.0 1.0 fusion.18
  (64 shorter events, 5.9 us)
Async XLA Ops:
  6.5 3.5 copy-start
  14.4 36.0 %all-to-all-start = ((bf16[8,48,24,128]{3,2,1,0:T(8,128)(2,1)}), bf16[8,48,24,128]{3,2,1,0:T(8,128)(2,1)S(1)}, u32[]{:S(2)}, u32[]{:S(2)}) async-start(bf16[8,48,24,128]{3,2,1,0:T(8,128)(2,1)} %stack.2), calls=%async_computation | async-start | bytes 4718592 | tf_op jit(solution)/shard_map/all_to_all | solution.py:126
  21.8 253.4 %reduce-scatter.2.cloned.1.call-start = ((), (), s32[]{:S(2)}) async-start(), calls=%async_computation.4 | async-start | bytes 10027008 | tf_op jit(solution)/shard_map/reduce_scatter | solution.py:131
  70.3 1.0 copy-start.2
  70.3 1.0 copy-start.9
  70.3 1.0 copy-start.12
  70.3 207.9 %copy-start.10 = (f32[128]{0:T(128)S(1)}, f32[128]{0:T(128)}, u32[]{:S(2)}) copy-start(f32[128]{0:T(128)} %param.19) | copy-start | bytes 1540
  70.3 209.4 %copy-start.4 = (bf16[128,128]{1,0:T(8,128)(2,1)S(1)}, bf16[128,128]{1,0:T(8,128)(2,1)}, u32[]{:S(2)}) copy-start(bf16[128,128]{1,0:T(8,128)(2,1)} %param.20) | copy-start | bytes 98308
  70.3 210.2 %copy-start.11 = (f32[128]{0:T(128)S(1)}, f32[128]{0:T(128)}, u32[]{:S(2)}) copy-start(f32[128]{0:T(128)} %param.21) | copy-start | bytes 1540
  70.3 211.3 %copy-start.8 = (bf16[128,4]{0,1:T(4,128)(2,1)S(1)}, bf16[128,4]{0,1:T(4,128)(2,1)}, u32[]{:S(2)}) copy-start(bf16[128,4]{0,1:T(4,128)(2,1)} %param.24) | copy-start | bytes 3076
  70.4 243.3 %copy-start.7 = (s32[4,4]{1,0:T(4,128)S(1)}, s32[4,4]{1,0:T(4,128)}, u32[]{:S(2)}) copy-start(s32[4,4]{1,0:T(4,128)} %param.15) | copy-start | bytes 196
  70.4 243.9 %copy-start.6 = (s32[384]{0:T(512)S(1)}, s32[384]{0:T(512)}, u32[]{:S(2)}) copy-start(s32[384]{0:T(512)} %param.14) | copy-start | bytes 4612
  70.4 254.4 %copy-start.3 = (bf16[128,384]{1,0:T(8,128)(2,1)S(1)}, bf16[128,384]{1,0:T(8,128)(2,1)}, u32[]{:S(2)}) copy-start(bf16[128,384]{1,0:T(8,128)(2,1)} %param.22) | copy-start | bytes 294916
  70.4 275.4 %all-gather.2.cloned.1.call-start = ((), (), s32[]{:S(2)}) async-start(), calls=%async_computation.5 | async-start | bytes 1327104 | tf_op jit(solution)/shard_map/all_gather | solution.py:24
  306.5 18.3 %all-to-all-start.1 = ((bf16[16,3,24,128]{3,2,1,0:T(8,128)(2,1)}), bf16[16,3,24,128]{3,2,1,0:T(8,128)(2,1)S(1)}, u32[]{:S(2)}, u32[]{:S(2)}) async-start(bf16[16,3,24,128]{3,2,1,0:T(8,128)(2,1)} %bitcast.6), calls=%async_computation.2 | async-start | bytes 589824 | tf_op jit(solution)/shard_map/all_to_all | solution.py:160
  379.3 4.0 copy-start.13
  379.3 21.8 %copy-start.5 = (bf16[128,128]{1,0:T(8,128)(2,1)S(1)}, bf16[128,128]{1,0:T(8,128)(2,1)}, u32[]{:S(2)}) copy-start(bf16[128,128]{1,0:T(8,128)(2,1)} %param.25) | copy-start | bytes 98308
  379.3 22.8 %copy-start.1 = (bf16[128,512]{1,0:T(8,128)(2,1)S(1)}, bf16[128,512]{1,0:T(8,128)(2,1)}, u32[]{:S(2)}) copy-start(bf16[128,512]{1,0:T(8,128)(2,1)} %param.17) | copy-start | bytes 393220
Sparse Core Ops, SparseCore 0:
  70.5 204.6 reduce-scatter.1
  306.6 39.1 all-gather.1
